TPU v7x, 512 devices: a whole 4x4x16 slice. The times are simulated.
512 devices in a mesh: seq: 32 (over z, core), table: 16 (over x, y).
Axes of the slice: x: 4, y: 4, z: 16, core: 2. Of those that a mesh axis runs over, the one named last changes fastest.
Arguments:
- columns: bfloat16 [16, 8192, 512], P(None, 'seq', 'table'), may hold values from -6 to 6
- gaps: float32 [16, 8192], P('table', 'seq'), may hold values from 0.2 to 9830.4
- norm_in: float32 [512], replicated, may hold values from 0.1 to 1.9
- w_gate: bfloat16 [512, 1024], replicated, may hold values from -0.25 to 0.25
- w_xbc: bfloat16 [512, 1280], replicated, may hold values from -0.25 to 0.25
- w_step: bfloat16 [512, 16], replicated, may hold values from -0.25 to 0.25
- step_bias: float32 [16], replicated, may hold values from -1 to 1
- conv_weight: float32 [4, 1280], replicated, may hold values from -1 to 1
- conv_bias: float32 [1280], replicated, may hold values from -1.5 to 1.5
- rates: float32 [16], replicated, may hold values from 6.1035156e-06 to 0.04
- norm_out: float32 [1024], replicated, may hold values from 0.1 to 1.9
- w_out: bfloat16 [1024, 512], replicated, may hold values from -0.1875 to 0.1875
Outputs:
- mixed: bfloat16 [16, 8192, 512], P('table', 'seq')
All inputs are finite; a program needn't handle non-finite values.
Results may differ from a plain program's by a relative error of at most 0.02.
Values may be sent and summed in bfloat16 or wider, within the bound.
No kernel may reach another device: no remote copies, remote signals or barrier semaphores. Data moves between devices by JAX's collectives and lax.ppermute only.
A program may use at most 64 MiB of HBM per device.

v0:
```python
import jax
import jax.numpy as jnp
from jax import lax
from jax.sharding import PartitionSpec as P

BLOCK = 256
epsilon = 1e-05


def passed_along(block, axis, distance):
    devices = range(lax.axis_size(axis))
    route = [(i - distance, i) for i in devices if i - distance in devices]
    return lax.ppermute(block, axis, route)


def rms_rows(values, gain):
    return values * lax.rsqrt(jnp.mean(values * values, axis=-1, keepdims=True) + epsilon) * gain


def block_terms(cx, cb, cc, cdt, cda):
    length = cx.shape[0]
    cs = jnp.cumsum(cda, axis=0)
    scores = jnp.dot(cc, cb.T, preferred_element_type=jnp.float32)
    trail = cs.T
    diff = trail[:, :, None] - trail[:, None, :]
    rows = lax.broadcasted_iota(jnp.int32, (length, length), 0)
    cols = lax.broadcasted_iota(jnp.int32, (length, length), 1)
    factor = jnp.exp(jnp.where((rows >= cols)[None], diff, -jnp.inf))
    mix = (scores[None] * factor * cdt.T[:, None, :]).astype(jnp.bfloat16)
    y_in = jnp.einsum("hts,shp->thp", mix, cx, preferred_element_type=jnp.float32)
    weighted = ((jnp.exp(cs[-1][None, :] - cs) * cdt)[:, :, None] * cx.astype(jnp.float32)).astype(
        jnp.bfloat16
    )
    block_state = jnp.einsum("shp,sn->hpn", weighted, cb, preferred_element_type=jnp.float32)
    return (y_in, block_state, cs)


def local_pass(xs, bm, cm, steps_dt, decay):
    length, heads, head_dim = xs.shape
    state_width = bm.shape[1]
    count = length // BLOCK
    blocks = (
        xs.reshape(count, BLOCK, heads, head_dim),
        bm.reshape(count, BLOCK, state_width),
        cm.reshape(count, BLOCK, state_width),
        steps_dt.reshape(count, BLOCK, heads),
        decay.reshape(count, BLOCK, heads),
    )

    def one_block(block):
        return block_terms(block[0], block[1], block[2], block[3], block[4])

    y_in, states, cs = lax.map(one_block, blocks)
    ends = cs[:, -1, :]

    def walk(state, paired):
        return (jnp.exp(paired[0])[:, None, None] * state + paired[1], state)

    final, entries = lax.scan(walk, jnp.zeros(states.shape[1:], jnp.float32), (ends, states))
    starts = jnp.cumsum(ends, axis=0) - ends
    total = jnp.sum(ends, axis=0)
    return (y_in, cs, entries, starts, final, total)


def carried_output(cm, cs, entries, starts, incoming):
    count, length = (cs.shape[0], cs.shape[1])
    queries = cm.reshape(count, length, cm.shape[1])
    enter = (entries + jnp.exp(starts)[:, :, None, None] * incoming[None]).astype(jnp.bfloat16)
    picked = jnp.einsum("ktn,khpn->kthp", queries, enter, preferred_element_type=jnp.float32)
    return jnp.exp(cs)[..., None] * picked


GROUP = 8


def parts_of(values):
    high = values.astype(jnp.bfloat16)
    rest = values - high.astype(jnp.float32)
    middle = rest.astype(jnp.bfloat16)
    low = (rest - middle.astype(jnp.float32)).astype(jnp.bfloat16)
    return jnp.stack([high, middle, low])


def within_groups(blocks):
    count = lax.axis_size("seq") // GROUP
    groups = [[g * GROUP + i for i in range(GROUP)] for g in range(count)]
    return lax.all_to_all(
        blocks, "seq", split_axis=0, concat_axis=0, tiled=True, axis_index_groups=groups
    )


def with_decay(state, logs):
    lead = state.shape[:-3]
    heads, head_dim, width = state.shape[-3:]
    rows = jnp.moveaxis(parts_of(logs), 0, -1).reshape(lead + (heads * 3, 1))
    rows = jnp.broadcast_to(rows, lead + (heads * 3, width))
    pad = [(0, 0)] * len(lead) + [(0, -(heads * 3) % 8), (0, 0)]
    flat = state.astype(jnp.bfloat16).reshape(lead + (heads * head_dim, width))
    return jnp.concatenate([flat, jnp.pad(rows, pad)], axis=-2)


def without_decay(block, heads):
    width = block.shape[-1]
    lead = block.shape[:-2]
    block = block.astype(jnp.float32)
    size = block.shape[-2] - heads * 3 - -(heads * 3) % 8
    state = block[..., :size, :].reshape(lead + (heads, size // heads, width))
    logs = block[..., size : size + heads * 3, 0].reshape(lead + (heads, 3)).sum(-1)
    return (state, logs)


def carry_in(total, final):
    heads, head_dim, width = final.shape
    own = heads // GROUP
    grouped = with_decay(final.reshape(GROUP, own, head_dim, width), total.reshape(GROUP, own))
    states, logs = without_decay(within_groups(grouped), own)
    prefix = [jnp.zeros_like(states[0])]
    before = [jnp.zeros_like(logs[0])]
    for member in range(GROUP):
        prefix.append(jnp.exp(logs[member])[:, None, None] * prefix[-1] + states[member])
        before.append(before[-1] + logs[member])
    block = with_decay(prefix[-1], before[-1])
    count = lax.axis_size("seq") // GROUP
    arrived = [
        without_decay(passed_along(block, "seq", GROUP * step), own) for step in range(1, count)
    ]
    enter = arrived[-1][0]
    for state, log in arrived[-2::-1]:
        enter = state + jnp.exp(log)[:, None, None] * enter
    back = jnp.stack(
        [prefix[member] + jnp.exp(before[member])[:, None, None] * enter for member in range(GROUP)]
    ).astype(jnp.bfloat16)
    return within_groups(back.reshape(GROUP, own * head_dim, width)).reshape(heads, head_dim, width)


def local(
    columns,
    gaps,
    norm_in,
    w_gate,
    w_xbc,
    w_step,
    step_bias,
    conv_weight,
    conv_bias,
    rates,
    norm_out,
    w_out,
):
    inner = w_gate.shape[1]
    heads = w_step.shape[1]
    head_dim = inner // heads
    state_width = (w_xbc.shape[1] - inner) // 2
    reach = conv_weight.shape[0] - 1
    normed = rms_rows(
        lax.all_to_all(columns, "table", split_axis=0, concat_axis=2, tiled=True).astype(
            jnp.float32
        ),
        norm_in,
    ).astype(jnp.bfloat16)
    gate = jnp.einsum("brd,de->bre", normed, w_gate, preferred_element_type=jnp.float32).astype(
        jnp.bfloat16
    )
    xbc = jnp.einsum("brd,de->bre", normed, w_xbc, preferred_element_type=jnp.float32).astype(
        jnp.bfloat16
    )
    step_raw = jnp.einsum("brd,de->bre", normed, w_step, preferred_element_type=jnp.float32)
    gate, xbc, step_raw, normed = (gate, xbc, step_raw, normed)
    hists, length = (xbc.shape[0], xbc.shape[1])
    rim = passed_along(xbc[:, length - reach :, :], "seq", 1)
    padded = jnp.concatenate([rim, xbc], axis=1).astype(jnp.float32)
    conv = conv_bias + conv_weight[0] * padded[:, 0:length]
    for offset in range(1, reach + 1):
        conv = conv + conv_weight[offset] * padded[:, offset : offset + length]
    act = jax.nn.silu(conv).astype(jnp.bfloat16)
    xs = act[:, :, :inner].reshape(hists, length, heads, head_dim)
    bm = act[:, :, inner : inner + state_width]
    cm = act[:, :, inner + state_width :]
    steps_dt = jax.nn.softplus(step_raw + step_bias)
    decay = -rates * steps_dt * gaps[:, :, None]
    y_in, cs, entries, starts, final, total = jax.vmap(local_pass)(xs, bm, cm, steps_dt, decay)
    incoming = carry_in(total[0], final[0])[None].astype(jnp.float32)
    state_terms = jax.vmap(carried_output)(cm, cs, entries, starts, incoming)
    y = (y_in + state_terms).reshape(hists, length, inner)
    gated = y * jax.nn.silu(gate.astype(jnp.float32))
    out_normed = rms_rows(gated, norm_out).astype(jnp.bfloat16)
    return jnp.einsum("bri,id->brd", out_normed, w_out, preferred_element_type=jnp.float32).astype(
        jnp.bfloat16
    )


def solution(mesh):
    in_specs = (
        P(None, "seq", "table"),
        P("table", "seq"),
        P(),
        P(),
        P(),
        P(),
        P(),
        P(),
        P(),
        P(),
        P(),
        P(),
    )
    out_specs = P("table", "seq", None)
    return jax.shard_map(local, mesh=mesh, in_specs=in_specs, out_specs=out_specs, check_vma=False)
```

profile of v0, /device:TPU:1, one launch (start us, length us, event | category | flops | bytes accessed | tf_op | source)
XLA Modules:
  0.0 95.5 jit_solution(16573989811518434025)
XLA Ops:
  0.0 7.7 %all-to-all-start = ((bf16[16,256,32]{1,2,0:T(8,128)(2,1)}), bf16[16,256,32]{1,2,0:T(8,128)(2,1)S(1)}, u32[]{:S(2)}, u32[]{:S(2)}) async-start(bf16[16,256,32]{1,2,0:T(8,128)(2,1)} %param.12), calls=%async_computation | async-start | bytes 524288 | tf_op jit(solution)/shard_map/all_to_all | solution.py:156
  7.8 0.7 neg.18
  8.4 0.9 slice_reduce_fusion.6
  9.4 5.8 %all-to-all-done = bf16[16,256,32]{1,2,0:T(8,128)(2,1)S(1)} async-done(((bf16[16,256,32]{1,2,0:T(8,128)(2,1)}), bf16[16,256,32]{1,2,0:T(8,128)(2,1)S(1)}, u32[]{:S(2)}, u32[]{:S(2)}) %all-to-all-start) | async-done | bytes 262176 | tf_op jit(solution)/shard_map/all_to_all | solution.py:156
  15.1 0.1 multiply_reduce_fusion.1
  15.3 0.8 fusion.22
  16.1 0.2 compare_select_fusion
  16.4 0.6 reduce-window.6
  16.9 0.2 slice_reduce_fusion
  17.1 0.1 copy.80
  17.3 0.6 exponential_bitcast_fusion
  18.0 0.2 slice_reduce_fusion.1
  18.2 0.5 fusion
  18.8 5.5 %collective-permute-start = (bf16[1,3,1280]{2,1,0:T(4,128)(2,1)S(1)}, bf16[1,3,1280]{2,1,0:T(4,128)(2,1)S(1)}, u32[]{:S(2)}, u32[]{:S(2)}) collective-permute-start(bf16[1,3,1280]{2,1,0:T(4,128)(2,1)S(1)} %slice.182), channel_id=1, source_target_pairs={{0,16},{16,32},{32,48},{48,64},{64,80},{80,96},{96,112},{112,128},... | collective-permute-start | bytes 23048 | tf_op jit(solution)/shard_map/ppermute | solution.py:13
  24.3 0.2 exponential_reduce_fusion
  24.7 1.1 %mul.674 = f32[256,16,64]{0,2,1:T(8,128)} broadcast(f32[256,16]{0,1:T(8,128)S(1)} %fusion.60), dimensions={0,1} | broadcast | bytes 1064960 | tf_op jit(solution)/shard_map/vmap()/while/body/eval_jaxpr/mul | solution.py:31
  25.8 1.6 %copy.82 = f32[1,256,1024]{2,1,0:T(8,128)S(1)} copy(f32[1,256,1024]{1,2,0:T(8,128)} %bitcast.196) | data formatting | bytes 2097152 | tf_op jit(solution)/shard_map/vmap()/while/body/eval_jaxpr/mul | solution.py:31
  27.4 0.1 copy.90
  27.5 0.1 reshape.878
  27.5 0.1 maximum_convert_fusion
  27.7 0.4 copy-done.4
  28.0 0.8 multiply_convert_fusion.4
  28.9 0.9 multiply_convert_fusion.6
  29.8 1.2 %copy.83 = bf16[1,256,1024]{1,2,0:T(8,128)(2,1)S(1)} copy(bf16[1,256,1024]{2,1,0:T(8,128)(2,1)} %multiply_convert_fusion.6) | data formatting | bytes 1048576 | tf_op jit(solution)/shard_map/vmap()/while/body/eval_jaxpr/convert_element_type | solution.py:31
  31.1 0.3 fusion.14
  31.5 16.6 %all_to_all.19 = bf16[8,136,128]{2,1,0:T(8,128)(2,1)S(1)} all-to-all(bf16[8,136,128]{2,1,0:T(8,128)(2,1)S(1)} %fusion.25), channel_id=1, replica_groups={{0,16,32,48,64,80,96,112},{128,144,160,176,192,208,224,240},{256,272,28..., dimensions={0} | all-to-all | bytes 557056 | tf_op jit(solution)/shard_map/all_to_all | solution.py:87
  48.1 0.1 copy.88
  48.4 0.4 exponential_reduce_fusion.1
  48.8 0.1 broadcast_in_dim.63
  49.0 0.1 mul.700
  49.3 0.1 mul.681
  49.5 0.1 mul.684
  49.8 0.1 mul.690
  50.1 0.1 mul.696
  50.2 0.2 fusion.29
  50.5 8.8 %collective-permute-start.1 = (bf16[136,128]{1,0:T(8,128)(2,1)S(1)}, bf16[136,128]{1,0:T(8,128)(2,1)S(1)}, u32[]{:S(2)}, u32[]{:S(2)}) collective-permute-start(bf16[136,128]{1,0:T(8,128)(2,1)S(1)} %pad_maximum_fusion), channel_id=1, source_target_pairs={{0,128},{16,144},{32,160},{48,176},{64,192},{80,208},{96,224},{112... | collective-permute-start | bytes 104456 | tf_op jit(solution)/shard_map/ppermute | solution.py:13
  59.3 5.4 %collective-permute-start.2 = (bf16[136,128]{1,0:T(8,128)(2,1)S(1)}, bf16[136,128]{1,0:T(8,128)(2,1)S(1)}, u32[]{:S(2)}, u32[]{:S(2)}) collective-permute-start(bf16[136,128]{1,0:T(8,128)(2,1)S(1)} %pad_maximum_fusion), channel_id=1, source_target_pairs={{0,256},{16,272},{32,288},{48,304},{64,320},{80,336},{96,352},{112... | collective-permute-start | bytes 104456 | tf_op jit(solution)/shard_map/ppermute | solution.py:13
  64.7 1.3 %collective-permute-start.3 = (bf16[136,128]{1,0:T(8,128)(2,1)S(1)}, bf16[136,128]{1,0:T(8,128)(2,1)S(1)}, u32[]{:S(2)}, u32[]{:S(2)}) collective-permute-start(bf16[136,128]{1,0:T(8,128)(2,1)S(1)} %pad_maximum_fusion), channel_id=1, source_target_pairs={{0,384},{16,400},{32,416},{48,432},{64,448},{80,464},{96,480},{112... | collective-permute-start | bytes 104456 | tf_op jit(solution)/shard_map/ppermute | solution.py:13
  67.1 0.1 slice_reduce_fusion.8
  67.3 0.1 slice_reduce_fusion.7
  67.5 0.1 reduce_sum.51
  67.8 0.1 reduce_sum.52
  68.1 2.2 %collective-permute-done.3 = bf16[136,128]{1,0:T(8,128)(2,1)S(1)} collective-permute-done((bf16[136,128]{1,0:T(8,128)(2,1)S(1)}, bf16[136,128]{1,0:T(8,128)(2,1)S(1)}, u32[]{:S(2)}, u32[]{:S(2)}) %collective-permute-start.3) | collective-permute-done | bytes 34848 | tf_op jit(solution)/shard_map/ppermute | solution.py:13
  70.3 0.7 bitcast_dynamic-update-slice_fusion
  71.0 0.7 fusion.53
  71.7 0.7 fusion.54
  72.5 0.7 fusion.55
  73.2 0.7 fusion.56
  73.9 0.7 fusion.57
  74.7 0.7 fusion.58
  75.4 0.7 fusion.59
  76.1 4.0 %all-to-all-start.2 = ((bf16[8,128,128]{2,1,0:T(8,128)(2,1)}), bf16[8,128,128]{2,1,0:T(8,128)(2,1)S(1)}, u32[]{:S(2)}, u32[]{:S(2)}) async-start(bf16[8,128,128]{2,1,0:T(8,128)(2,1)} %fusion.59), calls=%async_computation.2 | async-start | bytes 524288 | tf_op jit(solution)/shard_map/all_to_all | solution.py:87
  80.1 0.6 iota_compare_fusion.1
  80.9 0.7 mul.667
  81.6 0.6 bitcast_add_fusion.14
  82.2 0.2 copy.77
  82.5 0.2 fusion.46
  82.7 3.2 %fusion.8 = f32[256,16,64]{0,2,1:T(8,128)} fusion(bf16[256,16,64]{0,2,1:T(8,128)(2,1)S(1)} %bitcast.200, f32[16,256]{1,0:T(8,128)S(1)} %bitcast.201, f32[16,256]{1,0:T(8,128)} %bitcast_add_fusion.14, f32[256,256]{1,0:T(8,128)S(1)} %fusion.46, pred[256,256]{1,0:T(8,128)(4,1)} %iota_compare_fusion.1), kind=kOutput, calls=%fused_computation.10 | convolution fusion | flops 139460608 | bytes 1933312 | tf_op jit(solution)/shard_map/vmap()/while/body/eval_jaxpr/hts,shp->thp/dot_general | solution.py:30
  85.9 3.0 %all-to-all-done.2 = bf16[8,128,128]{2,1,0:T(8,128)(2,1)S(1)} async-done(((bf16[8,128,128]{2,1,0:T(8,128)(2,1)}), bf16[8,128,128]{2,1,0:T(8,128)(2,1)S(1)}, u32[]{:S(2)}, u32[]{:S(2)}) %all-to-all-start.2) | async-done | bytes 262176 | tf_op jit(solution)/shard_map/all_to_all | solution.py:87
  88.8 0.2 multiply_convert_fusion.8
  89.0 1.5 %fusion.9 = f32[256,16,64]{0,2,1:T(8,128)S(1)} fusion(f32[256,16,64]{0,2,1:T(8,128)} %fusion.8, bf16[16,64,128]{2,1,0:T(8,128)(2,1)S(1)} %bitcast.198, f32[256,16]{0,1:T(8,128)} %get-tuple-element.68, bf16[1,256,1280]{2,1,0:T(8,128)(2,1)S(1)} %multiply_convert_fusion.4), kind=kOutput, calls=%fused_computation.12 | convolution fusion | flops 67633152 | bytes 2441216 | tf_op jit(solution)/shard_map/vmap(ktn,khpn->kthp)/dot_general | solution.py:69
  90.6 1.3 %copy.89 = f32[256,1024]{1,0:T(8,128)} copy(f32[256,1024]{0,1:T(8,128)S(1)} %bitcast.195) | data formatting | bytes 2097152 | tf_op jit(solution)/shard_map/reshape | solution.py:184
  91.9 2.3 %multiply_reduce_fusion = (f32[256]{0:T(256)S(1)}, f32[256,1024]{1,0:T(8,128)S(1)}) fusion(f32[256,1024]{1,0:T(8,128)} %copy.89, bf16[256,512]{0,1:T(8,128)(2,1)S(1)} %fusion.22, bf16[512,1024]{1,0:T(8,128)(2,1)} %param.15), kind=kOutput, calls=%fused_computation.35 | convolution fusion | flops 270794496 | bytes 3408896 | tf_op jit(solution)/shard_map/brd,de->bre/dot_general | solution.py:161
  94.3 1.2 %fusion.15 = bf16[1,256,512]{2,1,0:T(8,128)(2,1)} fusion(bf16[1024,512]{1,0:T(8,128)(2,1)S(1)} %copy-done.1, f32[256,1024]{1,0:T(8,128)S(1)} %get-tuple-element.88, f32[1024]{0:T(1024)S(1)} %copy-done.5, f32[256]{0:T(256)S(1)} %add_rsqrt_fusion), kind=kOutput, calls=%fused_computation.28 | convolution fusion | flops 269352960 | bytes 2364416 | tf_op jit(solution)/shard_map/bri,id->brd/dot_general | solution.py:187
  (82 shorter events, 3.6 us)
Async XLA Ops:
  0.0 18.2 %copy-start = (bf16[512,1280]{1,0:T(8,128)(2,1)S(1)}, bf16[512,1280]{1,0:T(8,128)(2,1)}, u32[]{:S(2)}) copy-start(bf16[512,1280]{1,0:T(8,128)(2,1)} %param.16) | copy-start | bytes 3932164
  0.0 16.1 %copy-start.3 = (bf16[512,16]{0,1:T(8,128)(2,1)S(1)}, bf16[512,16]{0,1:T(8,128)(2,1)}, u32[]{:S(2)}) copy-start(bf16[512,16]{0,1:T(8,128)(2,1)} %param.17) | copy-start | bytes 49156
  0.0 16.1 %copy-start.7 = (f32[16]{0:T(128)S(1)}, f32[16]{0:T(128)}, u32[]{:S(2)}) copy-start(f32[16]{0:T(128)} %param.18) | copy-start | bytes 196
  0.0 16.3 %copy-start.6 = (f32[1,256]{1,0:T(1,128)S(1)}, f32[1,256]{1,0:T(1,128)}, u32[]{:S(2)}) copy-start(f32[1,256]{1,0:T(1,128)} %param.13) | copy-start | bytes 3076
  0.0 15.1 %all-to-all-start = ((bf16[16,256,32]{1,2,0:T(8,128)(2,1)}), bf16[16,256,32]{1,2,0:T(8,128)(2,1)S(1)}, u32[]{:S(2)}, u32[]{:S(2)}) async-start(bf16[16,256,32]{1,2,0:T(8,128)(2,1)} %param.12), calls=%async_computation | async-start | bytes 524288 | tf_op jit(solution)/shard_map/all_to_all | solution.py:156
  18.8 8.8 %collective-permute-start = (bf16[1,3,1280]{2,1,0:T(4,128)(2,1)S(1)}, bf16[1,3,1280]{2,1,0:T(4,128)(2,1)S(1)}, u32[]{:S(2)}, u32[]{:S(2)}) collective-permute-start(bf16[1,3,1280]{2,1,0:T(4,128)(2,1)S(1)} %slice.182), channel_id=1, source_target_pairs={{0,16},{16,32},{32,48},{48,64},{64,80},{80,96},{96,112},{112,128},... | collective-permute-start | bytes 23048 | tf_op jit(solution)/shard_map/ppermute | solution.py:13
  27.3 0.7 copy-start.4
  50.5 16.6 %collective-permute-start.1 = (bf16[136,128]{1,0:T(8,128)(2,1)S(1)}, bf16[136,128]{1,0:T(8,128)(2,1)S(1)}, u32[]{:S(2)}, u32[]{:S(2)}) collective-permute-start(bf16[136,128]{1,0:T(8,128)(2,1)S(1)} %pad_maximum_fusion), channel_id=1, source_target_pairs={{0,128},{16,144},{32,160},{48,176},{64,192},{80,208},{96,224},{112... | collective-permute-start | bytes 104456 | tf_op jit(solution)/shard_map/ppermute | solution.py:13
  59.3 7.9 %collective-permute-start.2 = (bf16[136,128]{1,0:T(8,128)(2,1)S(1)}, bf16[136,128]{1,0:T(8,128)(2,1)S(1)}, u32[]{:S(2)}, u32[]{:S(2)}) collective-permute-start(bf16[136,128]{1,0:T(8,128)(2,1)S(1)} %pad_maximum_fusion), channel_id=1, source_target_pairs={{0,256},{16,272},{32,288},{48,304},{64,320},{80,336},{96,352},{112... | collective-permute-start | bytes 104456 | tf_op jit(solution)/shard_map/ppermute | solution.py:13
  64.7 5.6 %collective-permute-start.3 = (bf16[136,128]{1,0:T(8,128)(2,1)S(1)}, bf16[136,128]{1,0:T(8,128)(2,1)S(1)}, u32[]{:S(2)}, u32[]{:S(2)}) collective-permute-start(bf16[136,128]{1,0:T(8,128)(2,1)S(1)} %pad_maximum_fusion), channel_id=1, source_target_pairs={{0,384},{16,400},{32,416},{48,432},{64,448},{80,464},{96,480},{112... | collective-permute-start | bytes 104456 | tf_op jit(solution)/shard_map/ppermute | solution.py:13
  76.1 12.7 %all-to-all-start.2 = ((bf16[8,128,128]{2,1,0:T(8,128)(2,1)}), bf16[8,128,128]{2,1,0:T(8,128)(2,1)S(1)}, u32[]{:S(2)}, u32[]{:S(2)}) async-start(bf16[8,128,128]{2,1,0:T(8,128)(2,1)} %fusion.59), calls=%async_computation.2 | async-start | bytes 524288 | tf_op jit(solution)/shard_map/all_to_all | solution.py:87
  82.6 6.2 %copy-start.2 = (f32[8,128]{1,0:T(8,128)S(1)}, f32[8,128]{1,0:T(8,128)}, u32[]{:S(2)}) copy-start(f32[8,128]{1,0:T(8,128)} %mul.667) | copy-start | bytes 12292
  91.9 2.4 %copy-start.1 = (bf16[1024,512]{1,0:T(8,128)(2,1)S(1)}, bf16[1024,512]{1,0:T(8,128)(2,1)}, u32[]{:S(2)}) copy-start(bf16[1024,512]{1,0:T(8,128)(2,1)} %param.23) | copy-start | bytes 3145732
  91.9 2.4 %copy-start.5 = (f32[1024]{0:T(1024)S(1)}, f32[1024]{0:T(1024)}, u32[]{:S(2)}) copy-start(f32[1024]{0:T(1024)} %param.22) | copy-start | bytes 12292
where the time goes:
time: 96.2 us; the launch traced here: 95.5 us
  starting transfers between devices  32.7 us (34%)
  blocking collectives  16.6 us (17%)
  other arithmetic  13.6 us (14%)
  local copies, waits for them, and re-layouts  11.8 us (12%)
  waiting for transfers between devices  11 us (11%)
  matrix products  9.44 us (10%)
    ppermute x4, starting transfers between devices, passed_along(): return lax.ppermute(block, axis, route)  21 us
    all_to_all x1, blocking collectives, within_groups(): lax.all_to_all(blocks, 'seq', split_axis=0, concat_axis=0, tiled=True, ax...  16.6 us
    all_to_all x1, starting transfers between devices, local(): lax.all_to_all(columns, 'table', split_axis=0, concat_axis=2, tiled=True)  7.73 us
    all_to_all x1, waiting for transfers between devices, local(): lax.all_to_all(columns, 'table', split_axis=0, concat_axis=2, tiled=True)  5.79 us
    unnamed x7, other arithmetic  5.08 us
    all_to_all x1, starting transfers between devices, within_groups(): lax.all_to_all(blocks, 'seq', split_axis=0, concat_axis=0, tiled=True, ax...  3.98 us
    dot_general x1, matrix products, block_terms(): jnp.einsum('hts,shp->thp', mix, cx, preferred_element_type=jnp.float32)  3.2 us
    all_to_all x1, waiting for transfers between devices, within_groups(): lax.all_to_all(blocks, 'seq', split_axis=0, concat_axis=0, tiled=True, ax...  2.97 us
  transfers between devices with their start and end apart: 6, of which 3 were waited for; matrix products, arithmetic and copies ran while one was open for 13% of the time, Pallas kernels for 0%

commit v1 on v0

--- a/solution.py
+++ b/solution.py
@@ -5,6 +5,12 @@
 
 BLOCK = 256
 epsilon = 1e-05
+
+
+def trade_parts(x, name, split, join):
+    cells = jnp.split(x, lax.axis_size(name), axis=split)
+    received = lax.all_to_all(jnp.stack(cells), name, 0, 0)
+    return jnp.concatenate(received, axis=join)
 
 
 def passed_along(block, axis, distance):
@@ -152,12 +158,9 @@
     head_dim = inner // heads
     state_width = (w_xbc.shape[1] - inner) // 2
     reach = conv_weight.shape[0] - 1
-    normed = rms_rows(
-        lax.all_to_all(columns, "table", split_axis=0, concat_axis=2, tiled=True).astype(
-            jnp.float32
-        ),
-        norm_in,
-    ).astype(jnp.bfloat16)
+    normed = rms_rows(trade_parts(columns, "table", 0, 2).astype(jnp.float32), norm_in).astype(
+        jnp.bfloat16
+    )
     gate = jnp.einsum("brd,de->bre", normed, w_gate, preferred_element_type=jnp.float32).astype(
         jnp.bfloat16
     )

time: 96.2 us -> 118 us (1.23); the launches traced: 95.5 us -> 116 us
  local copies, waits for them, and re-layouts: 11.8 us -> 33.1 us
    unnamed x16 -> x33, local copies, waits for them, and re-layouts: 0.38 us -> 20.3 us
    another operation x6 -> x7, local copies, waits for them, and re-layouts: 0.36 us -> 1.69 us  [the longest x1 1.32 us: trade_parts(): received = lax.all_to_all(jnp.stack(cells), name, 0, 0)]
  transfers between devices with their start and end apart: 6 -> 6, of which waited for: 3 -> 3; matrix products, arithmetic and copies ran while one was open for 13% -> 11% of each run, Pallas kernels for 0% -> 0%
where the time goes in v1:
time: 118 us; the launch traced here: 116 us
  local copies, waits for them, and re-layouts  33.1 us (28%)
  starting transfers between devices  32.6 us (28%)
  blocking collectives  16.6 us (14%)
  other arithmetic  12.9 us (11%)
  waiting for transfers between devices  11 us (9%)
  matrix products  9.43 us (8%)
    ppermute x4, starting transfers between devices, passed_along(): return lax.ppermute(block, axis, route)  21 us
    unnamed x33, local copies, waits for them, and re-layouts  20.3 us
    all_to_all x1, blocking collectives, within_groups(): lax.all_to_all(blocks, 'seq', split_axis=0, concat_axis=0, tiled=True, ax...  16.6 us
    all_to_all x1, starting transfers between devices, trade_parts(): received = lax.all_to_all(jnp.stack(cells), name, 0, 0)  7.58 us
    all_to_all x1, waiting for transfers between devices, trade_parts(): received = lax.all_to_all(jnp.stack(cells), name, 0, 0)  5.79 us
    unnamed x7, other arithmetic  5.08 us
    all_to_all x1, starting transfers between devices, within_groups(): lax.all_to_all(blocks, 'seq', split_axis=0, concat_axis=0, tiled=True, ax...  3.98 us
    dot_general x1, matrix products, block_terms(): jnp.einsum('hts,shp->thp', mix, cx, preferred_element_type=jnp.float32)  3.21 us
  transfers between devices with their start and end apart: 6, of which 3 were waited for; matrix products, arithmetic and copies ran while one was open for 11% of the time, Pallas kernels for 0%

profile of v1, /device:TPU:1, one launch (start us, length us, event | category | flops | bytes accessed | tf_op | source)
XLA Modules:
  0.0 115.9 jit_solution(3067642514187429369)
XLA Ops:
  0.0 1.4 %constant_dynamic-update-slice_fusion.15 = bf16[16,1,256,32]{2,3,1,0:T(8,128)(2,1)} fusion(bf16[16,256,32]{1,2,0:T(8,128)(2,1)} %param.12), kind=kLoop, calls=%fused_computation.113 | loop fusion | bytes 32768
  1.5 1.3 %constant_dynamic-update-slice_fusion.14 = bf16[16,1,256,32]{2,3,1,0:T(8,128)(2,1)} fusion(bf16[16,1,256,32]{2,3,1,0:T(8,128)(2,1)} %constant_dynamic-update-slice_fusion.15, bf16[16,256,32]{1,2,0:T(8,128)(2,1)} %param.12), kind=kLoop, calls=%fused_computation.112 | loop fusion | bytes 32768
  2.8 1.3 %constant_dynamic-update-slice_fusion.13 = bf16[16,1,256,32]{2,3,1,0:T(8,128)(2,1)} fusion(bf16[16,1,256,32]{2,3,1,0:T(8,128)(2,1)} %constant_dynamic-update-slice_fusion.14, bf16[16,256,32]{1,2,0:T(8,128)(2,1)} %param.12), kind=kLoop, calls=%fused_computation.111 | loop fusion | bytes 32768
  4.1 1.3 %constant_dynamic-update-slice_fusion.12 = bf16[16,1,256,32]{2,3,1,0:T(8,128)(2,1)} fusion(bf16[16,1,256,32]{2,3,1,0:T(8,128)(2,1)} %constant_dynamic-update-slice_fusion.13, bf16[16,256,32]{1,2,0:T(8,128)(2,1)} %param.12), kind=kLoop, calls=%fused_computation.110 | loop fusion | bytes 32768
  5.4 1.3 %constant_dynamic-update-slice_fusion.11 = bf16[16,1,256,32]{2,3,1,0:T(8,128)(2,1)} fusion(bf16[16,1,256,32]{2,3,1,0:T(8,128)(2,1)} %constant_dynamic-update-slice_fusion.12, bf16[16,256,32]{1,2,0:T(8,128)(2,1)} %param.12), kind=kLoop, calls=%fused_computation.109 | loop fusion | bytes 32768
  6.7 1.3 %constant_dynamic-update-slice_fusion.10 = bf16[16,1,256,32]{2,3,1,0:T(8,128)(2,1)} fusion(bf16[16,1,256,32]{2,3,1,0:T(8,128)(2,1)} %constant_dynamic-update-slice_fusion.11, bf16[16,256,32]{1,2,0:T(8,128)(2,1)} %param.12), kind=kLoop, calls=%fused_computation.108 | loop fusion | bytes 32768
  8.1 1.3 %constant_dynamic-update-slice_fusion.9 = bf16[16,1,256,32]{2,3,1,0:T(8,128)(2,1)} fusion(bf16[16,1,256,32]{2,3,1,0:T(8,128)(2,1)} %constant_dynamic-update-slice_fusion.10, bf16[16,256,32]{1,2,0:T(8,128)(2,1)} %param.12), kind=kLoop, calls=%fused_computation.107 | loop fusion | bytes 32768
  9.4 1.3 %constant_dynamic-update-slice_fusion.8 = bf16[16,1,256,32]{2,3,1,0:T(8,128)(2,1)} fusion(bf16[16,1,256,32]{2,3,1,0:T(8,128)(2,1)} %constant_dynamic-update-slice_fusion.9, bf16[16,256,32]{1,2,0:T(8,128)(2,1)} %param.12), kind=kLoop, calls=%fused_computation.106 | loop fusion | bytes 32768
  10.7 1.3 %constant_dynamic-update-slice_fusion.7 = bf16[16,1,256,32]{2,3,1,0:T(8,128)(2,1)} fusion(bf16[16,1,256,32]{2,3,1,0:T(8,128)(2,1)} %constant_dynamic-update-slice_fusion.8, bf16[16,256,32]{1,2,0:T(8,128)(2,1)} %param.12), kind=kLoop, calls=%fused_computation.105 | loop fusion | bytes 32768
  12.0 1.3 %constant_dynamic-update-slice_fusion.6 = bf16[16,1,256,32]{2,3,1,0:T(8,128)(2,1)} fusion(bf16[16,1,256,32]{2,3,1,0:T(8,128)(2,1)} %constant_dynamic-update-slice_fusion.7, bf16[16,256,32]{1,2,0:T(8,128)(2,1)} %param.12), kind=kLoop, calls=%fused_computation.104 | loop fusion | bytes 32768
  13.4 1.3 %constant_dynamic-update-slice_fusion.5 = bf16[16,1,256,32]{2,3,1,0:T(8,128)(2,1)} fusion(bf16[16,1,256,32]{2,3,1,0:T(8,128)(2,1)} %constant_dynamic-update-slice_fusion.6, bf16[16,256,32]{1,2,0:T(8,128)(2,1)} %param.12), kind=kLoop, calls=%fused_computation.103 | loop fusion | bytes 32768
  14.7 1.3 %constant_dynamic-update-slice_fusion.4 = bf16[16,1,256,32]{2,3,1,0:T(8,128)(2,1)} fusion(bf16[16,1,256,32]{2,3,1,0:T(8,128)(2,1)} %constant_dynamic-update-slice_fusion.5, bf16[16,256,32]{1,2,0:T(8,128)(2,1)} %param.12), kind=kLoop, calls=%fused_computation.102 | loop fusion | bytes 32768
  16.0 1.3 %constant_dynamic-update-slice_fusion.3 = bf16[16,1,256,32]{2,3,1,0:T(8,128)(2,1)} fusion(bf16[16,1,256,32]{2,3,1,0:T(8,128)(2,1)} %constant_dynamic-update-slice_fusion.4, bf16[16,256,32]{1,2,0:T(8,128)(2,1)} %param.12), kind=kLoop, calls=%fused_computation.101 | loop fusion | bytes 32768
  17.3 1.3 %constant_dynamic-update-slice_fusion.2 = bf16[16,1,256,32]{2,3,1,0:T(8,128)(2,1)} fusion(bf16[16,1,256,32]{2,3,1,0:T(8,128)(2,1)} %constant_dynamic-update-slice_fusion.3, bf16[16,256,32]{1,2,0:T(8,128)(2,1)} %param.12), kind=kLoop, calls=%fused_computation.100 | loop fusion | bytes 32768
  18.7 1.3 %constant_dynamic-update-slice_fusion.1 = bf16[16,1,256,32]{2,3,1,0:T(8,128)(2,1)} fusion(bf16[16,1,256,32]{2,3,1,0:T(8,128)(2,1)} %constant_dynamic-update-slice_fusion.2, bf16[16,256,32]{1,2,0:T(8,128)(2,1)} %param.12), kind=kLoop, calls=%fused_computation.99 | loop fusion | bytes 32768
  20.0 1.3 %constant_dynamic-update-slice_fusion = bf16[16,1,256,32]{2,3,1,0:T(8,128)(2,1)} fusion(bf16[16,1,256,32]{2,3,1,0:T(8,128)(2,1)} %constant_dynamic-update-slice_fusion.1, bf16[16,256,32]{1,2,0:T(8,128)(2,1)} %param.12), kind=kLoop, calls=%fused_computation.98 | loop fusion | bytes 32768 | tf_op jit(solution)/shard_map/stack | solution.py:12
  21.3 7.6 %all-to-all-start = ((bf16[16,1,256,32]{2,3,1,0:T(8,128)(2,1)}), bf16[16,1,256,32]{2,3,1,0:T(8,128)(2,1)S(1)}, u32[]{:S(2)}, u32[]{:S(2)}) async-start(bf16[16,1,256,32]{2,3,1,0:T(8,128)(2,1)} %constant_dynamic-update-slice_fusion), calls=%async_computation | async-start | bytes 524288 | tf_op jit(solution)/shard_map/all_to_all | solution.py:12
  28.9 0.7 neg.18
  29.6 0.9 slice_reduce_fusion.6
  30.5 5.8 %all-to-all-done = bf16[16,1,256,32]{2,3,1,0:T(8,128)(2,1)S(1)} async-done(((bf16[16,1,256,32]{2,3,1,0:T(8,128)(2,1)}), bf16[16,1,256,32]{2,3,1,0:T(8,128)(2,1)S(1)}, u32[]{:S(2)}, u32[]{:S(2)}) %all-to-all-start) | async-done | bytes 262176 | tf_op jit(solution)/shard_map/all_to_all | solution.py:12
  36.6 0.2 compare_select_fusion
  36.8 0.6 reduce-window.6
  37.4 0.2 slice_reduce_fusion
  37.8 0.6 exponential_bitcast_fusion
  38.4 0.2 slice_reduce_fusion.1
  38.7 0.5 fusion
  39.2 5.5 %collective-permute-start = (bf16[1,3,1280]{2,1,0:T(4,128)(2,1)S(1)}, bf16[1,3,1280]{2,1,0:T(4,128)(2,1)S(1)}, u32[]{:S(2)}, u32[]{:S(2)}) collective-permute-start(bf16[1,3,1280]{2,1,0:T(4,128)(2,1)S(1)} %slice.182), channel_id=1, source_target_pairs={{0,16},{16,32},{32,48},{48,64},{64,80},{80,96},{96,112},{112,128},... | collective-permute-start | bytes 23048 | tf_op jit(solution)/shard_map/ppermute | solution.py:19
  44.8 0.2 exponential_reduce_fusion
  45.2 1.1 mul.673
  46.2 1.6 %copy.82 = f32[1,256,1024]{2,1,0:T(8,128)S(1)} copy(f32[1,256,1024]{1,2,0:T(8,128)} %bitcast.226) | data formatting | bytes 2097152 | tf_op jit(solution)/shard_map/vmap()/while/body/eval_jaxpr/mul | solution.py:37
  48.0 0.1 maximum_convert_fusion
  48.2 0.4 copy-done.4
  48.5 0.8 multiply_convert_fusion.4
  49.3 0.9 multiply_convert_fusion.6
  50.3 1.2 %copy.83 = bf16[1,256,1024]{1,2,0:T(8,128)(2,1)S(1)} copy(bf16[1,256,1024]{2,1,0:T(8,128)(2,1)} %multiply_convert_fusion.6) | data formatting | bytes 1048576 | tf_op jit(solution)/shard_map/vmap()/while/body/eval_jaxpr/convert_element_type | solution.py:37
  51.5 0.3 fusion.14
  51.9 16.6 %all_to_all.15 = bf16[8,136,128]{2,1,0:T(8,128)(2,1)S(1)} all-to-all(bf16[8,136,128]{2,1,0:T(8,128)(2,1)S(1)} %fusion.25), channel_id=1, replica_groups={{0,16,32,48,64,80,96,112},{128,144,160,176,192,208,224,240},{256,272,28..., dimensions={0} | all-to-all | bytes 557056 | tf_op jit(solution)/shard_map/all_to_all | solution.py:93
  68.8 0.4 exponential_reduce_fusion.1
  70.7 0.2 fusion.29
  71.0 8.8 %collective-permute-start.1 = (bf16[136,128]{1,0:T(8,128)(2,1)S(1)}, bf16[136,128]{1,0:T(8,128)(2,1)S(1)}, u32[]{:S(2)}, u32[]{:S(2)}) collective-permute-start(bf16[136,128]{1,0:T(8,128)(2,1)S(1)} %pad_maximum_fusion), channel_id=1, source_target_pairs={{0,128},{16,144},{32,160},{48,176},{64,192},{80,208},{96,224},{112... | collective-permute-start | bytes 104456 | tf_op jit(solution)/shard_map/ppermute | solution.py:19
  79.8 5.4 %collective-permute-start.2 = (bf16[136,128]{1,0:T(8,128)(2,1)S(1)}, bf16[136,128]{1,0:T(8,128)(2,1)S(1)}, u32[]{:S(2)}, u32[]{:S(2)}) collective-permute-start(bf16[136,128]{1,0:T(8,128)(2,1)S(1)} %pad_maximum_fusion), channel_id=1, source_target_pairs={{0,256},{16,272},{32,288},{48,304},{64,320},{80,336},{96,352},{112... | collective-permute-start | bytes 104456 | tf_op jit(solution)/shard_map/ppermute | solution.py:19
  85.2 1.3 %collective-permute-start.3 = (bf16[136,128]{1,0:T(8,128)(2,1)S(1)}, bf16[136,128]{1,0:T(8,128)(2,1)S(1)}, u32[]{:S(2)}, u32[]{:S(2)}) collective-permute-start(bf16[136,128]{1,0:T(8,128)(2,1)S(1)} %pad_maximum_fusion), channel_id=1, source_target_pairs={{0,384},{16,400},{32,416},{48,432},{64,448},{80,464},{96,480},{112... | collective-permute-start | bytes 104456 | tf_op jit(solution)/shard_map/ppermute | solution.py:19
  88.6 2.2 %collective-permute-done.3 = bf16[136,128]{1,0:T(8,128)(2,1)S(1)} collective-permute-done((bf16[136,128]{1,0:T(8,128)(2,1)S(1)}, bf16[136,128]{1,0:T(8,128)(2,1)S(1)}, u32[]{:S(2)}, u32[]{:S(2)}) %collective-permute-start.3) | collective-permute-done | bytes 34848 | tf_op jit(solution)/shard_map/ppermute | solution.py:19
  90.8 0.7 constant_dynamic-update-slice_fusion.23
  91.5 0.7 constant_dynamic-update-slice_fusion.22
  92.2 0.7 constant_dynamic-update-slice_fusion.21
  92.9 0.7 constant_dynamic-update-slice_fusion.20
  93.7 0.7 constant_dynamic-update-slice_fusion.19
  94.4 0.7 constant_dynamic-update-slice_fusion.18
  95.1 0.7 constant_dynamic-update-slice_fusion.17
  95.8 0.7 constant_dynamic-update-slice_fusion.16
  96.6 4.0 %all-to-all-start.2 = ((bf16[8,128,128]{2,1,0:T(8,128)(2,1)}), bf16[8,128,128]{2,1,0:T(8,128)(2,1)S(1)}, u32[]{:S(2)}, u32[]{:S(2)}) async-start(bf16[8,128,128]{2,1,0:T(8,128)(2,1)} %constant_dynamic-update-slice_fusion.16), calls=%async_computation.2 | async-start | bytes 524288 | tf_op jit(solution)/shard_map/all_to_all | solution.py:93
  100.6 0.6 iota_compare_fusion.1
  101.4 0.7 mul.666
  102.0 0.6 bitcast_add_fusion.14
  102.7 0.2 copy.77
  102.9 0.2 fusion.46
  103.1 3.2 %fusion.8 = f32[256,16,64]{0,2,1:T(8,128)} fusion(bf16[256,16,64]{0,2,1:T(8,128)(2,1)S(1)} %bitcast.230, f32[16,256]{1,0:T(8,128)S(1)} %bitcast.231, f32[16,256]{1,0:T(8,128)} %bitcast_add_fusion.14, f32[256,256]{1,0:T(8,128)S(1)} %fusion.46, pred[256,256]{1,0:T(8,128)(4,1)} %iota_compare_fusion.1), kind=kOutput, calls=%fused_computation.10 | convolution fusion | flops 139460608 | bytes 1933312 | tf_op jit(solution)/shard_map/vmap()/while/body/eval_jaxpr/hts,shp->thp/dot_general | solution.py:36
  106.3 3.0 %all-to-all-done.2 = bf16[8,128,128]{2,1,0:T(8,128)(2,1)S(1)} async-done(((bf16[8,128,128]{2,1,0:T(8,128)(2,1)}), bf16[8,128,128]{2,1,0:T(8,128)(2,1)S(1)}, u32[]{:S(2)}, u32[]{:S(2)}) %all-to-all-start.2) | async-done | bytes 262176 | tf_op jit(solution)/shard_map/all_to_all | solution.py:93
  109.3 0.2 multiply_convert_fusion.8
  109.5 1.5 %fusion.9 = f32[256,16,64]{0,2,1:T(8,128)S(1)} fusion(f32[256,16,64]{0,2,1:T(8,128)} %fusion.8, bf16[16,64,128]{2,1,0:T(8,128)(2,1)S(1)} %bitcast.228, f32[256,16]{0,1:T(8,128)} %get-tuple-element.68, bf16[1,256,1280]{2,1,0:T(8,128)(2,1)S(1)} %multiply_convert_fusion.4), kind=kOutput, calls=%fused_computation.12 | convolution fusion | flops 67633152 | bytes 2441216 | tf_op jit(solution)/shard_map/vmap(ktn,khpn->kthp)/dot_general | solution.py:75
  111.0 1.3 %copy.89 = f32[256,1024]{1,0:T(8,128)} copy(f32[256,1024]{0,1:T(8,128)S(1)} %bitcast.225) | data formatting | bytes 2097152 | tf_op jit(solution)/shard_map/reshape | solution.py:187
  112.3 2.3 %multiply_reduce_fusion = (f32[256]{0:T(256)S(1)}, f32[256,1024]{1,0:T(8,128)S(1)}) fusion(f32[256,1024]{1,0:T(8,128)} %copy.89, bf16[256,512]{0,1:T(8,128)(2,1)S(1)} %fusion.22, bf16[512,1024]{1,0:T(8,128)(2,1)} %param.15), kind=kOutput, calls=%fused_computation.35 | convolution fusion | flops 270794496 | bytes 3408896 | tf_op jit(solution)/shard_map/brd,de->bre/dot_general | solution.py:164
  114.7 1.2 %fusion.15 = bf16[1,256,512]{2,1,0:T(8,128)(2,1)} fusion(bf16[1024,512]{1,0:T(8,128)(2,1)S(1)} %copy-done.1, f32[256,1024]{1,0:T(8,128)S(1)} %get-tuple-element.88, f32[1024]{0:T(1024)S(1)} %copy-done.5, f32[256]{0:T(256)S(1)} %add_rsqrt_fusion), kind=kOutput, calls=%fused_computation.28 | convolution fusion | flops 269352960 | bytes 2364416 | tf_op jit(solution)/shard_map/bri,id->brd/dot_general | solution.py:190
  (100 shorter events, 5.2 us)
Async XLA Ops:
  0.0 38.7 %copy-start = (bf16[512,1280]{1,0:T(8,128)(2,1)S(1)}, bf16[512,1280]{1,0:T(8,128)(2,1)}, u32[]{:S(2)}) copy-start(bf16[512,1280]{1,0:T(8,128)(2,1)} %param.16) | copy-start | bytes 3932164
  0.0 36.4 %copy-start.6 = (f32[512]{0:T(512)S(1)}, f32[512]{0:T(512)}, u32[]{:S(2)}) copy-start(f32[512]{0:T(512)} %param.14) | copy-start | bytes 6148
  0.0 36.5 %copy-start.3 = (bf16[512,16]{0,1:T(8,128)(2,1)S(1)}, bf16[512,16]{0,1:T(8,128)(2,1)}, u32[]{:S(2)}) copy-start(bf16[512,16]{0,1:T(8,128)(2,1)} %param.17) | copy-start | bytes 49156
  0.0 36.5 %copy-start.8 = (f32[16]{0:T(128)S(1)}, f32[16]{0:T(128)}, u32[]{:S(2)}) copy-start(f32[16]{0:T(128)} %param.18) | copy-start | bytes 196
  0.0 36.7 %copy-start.7 = (f32[1,256]{1,0:T(1,128)S(1)}, f32[1,256]{1,0:T(1,128)}, u32[]{:S(2)}) copy-start(f32[1,256]{1,0:T(1,128)} %param.13) | copy-start | bytes 3076
  21.3 15.0 %all-to-all-start = ((bf16[16,1,256,32]{2,3,1,0:T(8,128)(2,1)}), bf16[16,1,256,32]{2,3,1,0:T(8,128)(2,1)S(1)}, u32[]{:S(2)}, u32[]{:S(2)}) async-start(bf16[16,1,256,32]{2,3,1,0:T(8,128)(2,1)} %constant_dynamic-update-slice_fusion), calls=%async_computation | async-start | bytes 524288 | tf_op jit(solution)/shard_map/all_to_all | solution.py:12
  39.2 8.8 %collective-permute-start = (bf16[1,3,1280]{2,1,0:T(4,128)(2,1)S(1)}, bf16[1,3,1280]{2,1,0:T(4,128)(2,1)S(1)}, u32[]{:S(2)}, u32[]{:S(2)}) collective-permute-start(bf16[1,3,1280]{2,1,0:T(4,128)(2,1)S(1)} %slice.182), channel_id=1, source_target_pairs={{0,16},{16,32},{32,48},{48,64},{64,80},{80,96},{96,112},{112,128},... | collective-permute-start | bytes 23048 | tf_op jit(solution)/shard_map/ppermute | solution.py:19
  47.8 0.7 copy-start.4
  71.0 16.6 %collective-permute-start.1 = (bf16[136,128]{1,0:T(8,128)(2,1)S(1)}, bf16[136,128]{1,0:T(8,128)(2,1)S(1)}, u32[]{:S(2)}, u32[]{:S(2)}) collective-permute-start(bf16[136,128]{1,0:T(8,128)(2,1)S(1)} %pad_maximum_fusion), channel_id=1, source_target_pairs={{0,128},{16,144},{32,160},{48,176},{64,192},{80,208},{96,224},{112... | collective-permute-start | bytes 104456 | tf_op jit(solution)/shard_map/ppermute | solution.py:19
  79.8 7.9 %collective-permute-start.2 = (bf16[136,128]{1,0:T(8,128)(2,1)S(1)}, bf16[136,128]{1,0:T(8,128)(2,1)S(1)}, u32[]{:S(2)}, u32[]{:S(2)}) collective-permute-start(bf16[136,128]{1,0:T(8,128)(2,1)S(1)} %pad_maximum_fusion), channel_id=1, source_target_pairs={{0,256},{16,272},{32,288},{48,304},{64,320},{80,336},{96,352},{112... | collective-permute-start | bytes 104456 | tf_op jit(solution)/shard_map/ppermute | solution.py:19
  85.2 5.6 %collective-permute-start.3 = (bf16[136,128]{1,0:T(8,128)(2,1)S(1)}, bf16[136,128]{1,0:T(8,128)(2,1)S(1)}, u32[]{:S(2)}, u32[]{:S(2)}) collective-permute-start(bf16[136,128]{1,0:T(8,128)(2,1)S(1)} %pad_maximum_fusion), channel_id=1, source_target_pairs={{0,384},{16,400},{32,416},{48,432},{64,448},{80,464},{96,480},{112... | collective-permute-start | bytes 104456 | tf_op jit(solution)/shard_map/ppermute | solution.py:19
  96.6 12.7 %all-to-all-start.2 = ((bf16[8,128,128]{2,1,0:T(8,128)(2,1)}), bf16[8,128,128]{2,1,0:T(8,128)(2,1)S(1)}, u32[]{:S(2)}, u32[]{:S(2)}) async-start(bf16[8,128,128]{2,1,0:T(8,128)(2,1)} %constant_dynamic-update-slice_fusion.16), calls=%async_computation.2 | async-start | bytes 524288 | tf_op jit(solution)/shard_map/all_to_all | solution.py:93
  103.1 6.2 %copy-start.2 = (f32[8,128]{1,0:T(8,128)S(1)}, f32[8,128]{1,0:T(8,128)}, u32[]{:S(2)}) copy-start(f32[8,128]{1,0:T(8,128)} %mul.666) | copy-start | bytes 12292
  112.3 2.4 %copy-start.1 = (bf16[1024,512]{1,0:T(8,128)(2,1)S(1)}, bf16[1024,512]{1,0:T(8,128)(2,1)}, u32[]{:S(2)}) copy-start(bf16[1024,512]{1,0:T(8,128)(2,1)} %param.23) | copy-start | bytes 3145732
  112.3 2.4 %copy-start.5 = (f32[1024]{0:T(1024)S(1)}, f32[1024]{0:T(1024)}, u32[]{:S(2)}) copy-start(f32[1024]{0:T(1024)} %param.22) | copy-start | bytes 12292
